TPU v7x, 32 devices: a whole 2x2x4 slice. The times are simulated.
32 devices in a mesh: wide: 8 (over z, y), narrow: 4 (over x, core).
Axes of the slice: x: 2, y: 2, z: 4, core: 2. Of those that a mesh axis runs over, the one named last changes fastest.
Arguments:
- prior_lt: float32 [4096, 6144], P('narrow', 'wide'), may hold values from -2 to 2
- prior_d: float32 [4096], P('narrow'), may hold values from -4 to 4
- prior_e: float32 [4096], P('narrow'), may hold values from -4 to 4
- prior_pairs: int32 [4096], P('narrow'), may hold values from 0 to 1, as said below
- pivots: int32 [2, 256], replicated, may hold values from 0 to 6143, as said below
- a_first: float32 [256, 6144], P('narrow', 'wide'), may hold values from -6 to 6
- a_second: float32 [256, 6144], P('narrow', 'wide'), may hold values from -6 to 6
- inv_d: float32 [2, 256], P(None, 'narrow'), may hold values from -4 to 4
- inv_e: float32 [2, 256], P(None, 'narrow'), may hold values from -4 to 4
- panel_pairs: int32 [2, 256], P(None, 'narrow'), may hold values from 0 to 1, as said below
Outputs:
- l_first: float32 [256, 6144], P('narrow', 'wide')
- l_second: float32 [256, 6144], P('narrow', 'wide')
Inputs may be any that keep to these rules, and one draw needn't show every extreme that they name: `pivots`: all 512 pivot rows are distinct; at most 128 of them lie in one tile of 768 consecutive rows, and some tile holds exactly 128. `prior_pairs`: 1 only at even positions; a 1 at position k joins k and k + 1 into a 2 x 2 pivot block. `panel_pairs`: 1 only at even positions along the last dimension; a 1 at position k joins k and k + 1 into a 2 x 2 pivot block.
All inputs are finite; a program needn't handle non-finite values.
Results may differ from a plain program's by a relative error of at most 0.000098.
Values sent between devices are 32-bit elements; how exact they have to be, the bound alone decides.
A program may use at most 64 MiB of HBM per device.

v0:
```python
import jax
import jax.numpy as jnp
from jax import lax
from jax.sharding import PartitionSpec as P

P_SIZE = 256


def couple(block, diag, off, pairs):
    joined = off * pairs.astype(jnp.float32)
    zero_row = jnp.zeros_like(block[:1])
    after = jnp.concatenate([block[1:], zero_row], 0)
    before = jnp.concatenate([zero_row, block[:-1]], 0)
    lower = jnp.concatenate([jnp.zeros_like(joined[:1]), joined[:-1]], 0)
    return diag[:, None] * block + joined[:, None] * after + lower[:, None] * before


def slot_layout(targets, tile_rows, capacity):
    owner = targets // tile_rows
    count = targets.shape[0]
    order = jnp.arange(count)
    same = (owner[:, None] == owner[None, :]) & (order[:, None] > order[None, :])
    rank = jnp.sum(same.astype(jnp.int32), axis=1)
    return (owner, rank, owner * capacity + rank)


def pack_local(block, targets, owner, rank, here, tile_rows, capacity):
    hit = (owner[None, :] == here) & (rank[None, :] == jnp.arange(capacity)[:, None])
    local_index = jnp.sum(jnp.where(hit, (targets % tile_rows)[None, :], 0), axis=1)
    valid = jnp.any(hit, axis=1)
    taken = jnp.take(block, local_index, axis=1)
    return jnp.where(valid[None, :], taken, 0.0)


def shards(
    prior_lt, prior_d, prior_e, prior_pairs, pivots, a_first, a_second, inv_d, inv_e, panel_pairs
):
    k_local, tile_rows = prior_lt.shape
    blocks = a_first.shape[0]
    narrow_count = lax.axis_size("narrow")
    here = lax.axis_index("wide")
    capacity = max(4 * P_SIZE // lax.axis_size("wide"), 2)
    flat = pivots.reshape(-1)
    second = pivots[1]
    owner, rank, slot = slot_layout(flat, tile_rows, capacity)
    packed = pack_local(prior_lt, flat, owner, rank, here, tile_rows, capacity)
    gathered = lax.all_gather(packed, "wide", axis=1, tiled=True)
    chosen = jnp.take(gathered, slot, axis=1)
    coupled = couple(chosen, prior_d, prior_e, prior_pairs)
    arranged = (
        coupled.reshape(k_local, 2, narrow_count, blocks)
        .transpose(0, 2, 1, 3)
        .reshape(k_local, 2 * P_SIZE)
    )
    columns = arranged
    update = lax.psum_scatter(
        lax.dot_general(
            columns, prior_lt, (((0,), (0,)), ((), ())), precision=lax.Precision.HIGHEST
        ),
        "narrow",
        scatter_dimension=0,
        tiled=True,
    )
    w_first = a_first - update[:blocks]
    l_first = couple(w_first, inv_d[0], inv_e[0], panel_pairs[0])
    owner_two, rank_two, slot_two = slot_layout(second, tile_rows, capacity)
    packed_two = pack_local(l_first, second, owner_two, rank_two, here, tile_rows, capacity)
    gathered_two = lax.all_gather(packed_two, "wide", axis=1, tiled=True)
    crossed = jnp.take(gathered_two, slot_two, axis=1)
    columns = crossed
    correction = lax.psum_scatter(
        lax.dot_general(
            columns, w_first, (((0,), (0,)), ((), ())), precision=lax.Precision.HIGHEST
        ),
        "narrow",
        scatter_dimension=0,
        tiled=True,
    )
    w_second = a_second - update[blocks:] - correction
    l_second = couple(w_second, inv_d[1], inv_e[1], panel_pairs[1])
    return (l_first, l_second)


def solution(mesh):
    in_specs = (
        P("narrow", "wide"),
        P("narrow"),
        P("narrow"),
        P("narrow"),
        P(),
        P("narrow", "wide"),
        P("narrow", "wide"),
        P(None, "narrow"),
        P(None, "narrow"),
        P(None, "narrow"),
    )
    out_specs = (P("narrow", "wide"), P("narrow", "wide"))
    return jax.shard_map(shards, mesh=mesh, in_specs=in_specs, out_specs=out_specs, check_vma=False)
```

profile of v0, /device:TPU:0, one launch (start us, length us, event | category | flops | bytes accessed | tf_op | source)
XLA Modules:
  0.0 200.7 jit_solution(961543816702302315)
XLA Ops:
  7.2 0.0 all-gather.2.cloned.1.call-start
  7.2 0.7 broadcast_divide_fusion
  7.9 0.7 and_bitcast_fusion
  8.7 0.2 convert_reduce_fusion
  8.9 0.1 select_reduce_fusion
  9.1 0.1 fusion.2
  9.2 2.4 %copy.17 = f32[1024,768]{0,1:T(8,128)S(1)} copy(f32[1024,768]{1,0:T(8,128)} %param.10) | data formatting | bytes 6291456 | tf_op args[0]
  11.6 0.0 copy-start.7
  11.6 0.0 copy-start.8
  11.6 1.6 gather_fusion
  13.2 2.0 select_bitcast_fusion.1
  15.2 0.0 all-gather.2.cloned.1.call-update
  15.2 0.0 reduce-scatter.3.cloned.1.call-start
  15.3 0.1 pad_maximum_fusion
  15.4 75.4 %all-gather.2.cloned.1.call-done = f32[1024,1024]{0,1:T(8,128)} async-done(((f32[1024,128]{0,1:T(8,128)}), f32[1024,1024]{0,1:T(8,128)}) %all-gather.2.cloned.1.call-update) | async-done | bytes 4194320 | tf_op jit(solution)/shard_map/all_gather | solution.py:47
  90.9 5.0 %gather_fusion.1 = f32[512,1024]{1,0:T(8,128)S(1)} fusion(f32[1024,1024]{0,1:T(8,128)} %all-gather.2.cloned.1.call-done, s32[1024]{0:T(1024)S(1)} %pad_clamp_fusion.2), kind=kCustom, calls=%fused_computation.1 | custom fusion | bytes 4196352 | tf_op jit(solution)/shard_map/jit(_take)/gather | solution.py:48
  95.9 0.2 select_bitcast_fusion
  96.1 0.0 copy-start.6
  96.1 0.8 fusion.18
  97.0 0.8 multiply_add_fusion
  97.8 0.0 copy-start
  97.8 0.1 copy.18
  97.9 1.7 copy-done
  99.7 0.0 copy-start.3
  99.7 6.4 %fusion.21 = f32[512,768]{1,0:T(8,128)} fusion(f32[1024,512]{0,1:T(8,128)S(1)} %bitcast.68, f32[1024,768]{1,0:T(8,128)S(1)} %copy-done), kind=kOutput, calls=%fused_computation.83 | convolution fusion | flops 4831838208 | bytes 6815744 | tf_op jit(solution)/shard_map/dot_general | solution.py:57
  106.1 0.0 reduce-scatter.3.cloned.1.call-update
  106.1 0.0 reduce-scatter.5.cloned.1.call-start
  106.3 0.0 copy-done.9
  106.3 0.1 pad_maximum_fusion.2
  106.4 0.2 convert_reduce_fusion.1
  106.6 0.1 select_reduce_fusion.1
  106.8 0.1 fusion.8
  106.9 25.9 %reduce-scatter.3.cloned.1.call-done = f32[128,768]{1,0:T(8,128)} async-done(((f32[512,768]{1,0:T(8,128)}), f32[128,768]{1,0:T(8,128)}) %reduce-scatter.3.cloned.1.call-update) | async-done | bytes 393232 | tf_op jit(solution)/shard_map/reduce_scatter | solution.py:56
  132.9 0.9 slice_subtract_fusion.1
  133.9 0.1 multiply_add_fusion.2
  134.0 0.0 copy-start.1
  134.0 0.0 copy-start.4
  134.0 0.2 copy.19
  134.2 0.6 gather_fusion.2
  134.8 0.1 select_bitcast_fusion.2
  134.9 31.5 %all_gather.7 = f32[64,1024]{0,1:T(8,128)S(1)} all-gather(f32[64,128]{0,1:T(8,128)S(1)} %select_bitcast_fusion.2), channel_id=1, replica_groups=mesh['wide'=8,'narrow'=4] {'wide'}, dimensions={1}, use_global_device_ids=true | all-gather | bytes 294912 | tf_op jit(solution)/shard_map/all_gather | solution.py:68
  166.4 0.7 gather_fusion.3
  167.2 1.7 fusion.5
  168.9 0.0 reduce-scatter.5.cloned.1.call-update
  168.9 0.1 pad_maximum_fusion.1
  169.0 23.3 %reduce-scatter.5.cloned.1.call-done = f32[64,768]{1,0:T(8,128)} async-done(((f32[256,768]{1,0:T(8,128)}), f32[64,768]{1,0:T(8,128)}) %reduce-scatter.5.cloned.1.call-update) | async-done | bytes 196624 | tf_op jit(solution)/shard_map/reduce_scatter | solution.py:71
  192.3 1.0 fusion.4
  193.3 0.8 multiply_add_fusion.1
  (45 shorter events, 0.3 us)
Async XLA Ops:
  7.2 83.7 %all-gather.2.cloned.1.call-start = ((), (), s32[]{:S(2)}) async-start(), calls=%async_computation.2 | async-start | bytes 4718592 | tf_op jit(solution)/shard_map/all_gather | solution.py:47
  11.6 3.7 %copy-start.7 = (f32[1024]{0:T(1024)S(1)}, f32[1024]{0:T(1024)}, u32[]{:S(2)}) copy-start(f32[1024]{0:T(1024)} %param.12) | copy-start | bytes 12292
  11.6 3.7 %copy-start.8 = (s32[1024]{0:T(1024)S(1)}, s32[1024]{0:T(1024)}, u32[]{:S(2)}) copy-start(s32[1024]{0:T(1024)} %param.13) | copy-start | bytes 12292
  15.2 117.7 %reduce-scatter.3.cloned.1.call-start = ((), (), s32[]{:S(2)}) async-start(), calls=%async_computation.3 | async-start | bytes 1966080 | tf_op jit(solution)/shard_map/reduce_scatter | solution.py:56
  96.1 0.9 copy-start.6
  97.8 1.9 copy-start
  99.7 6.5 %copy-start.5 = (s32[2,256]{1,0:T(2,128)S(1)}, s32[2,256]{1,0:T(2,128)}, u32[]{:S(2)}) copy-start(s32[2,256]{1,0:T(2,128)} %param.14) | copy-start | bytes 6148
  99.7 6.6 %copy-start.9 = (s32[2,64]{1,0:T(2,128)S(1)}, s32[2,64]{1,0:T(2,128)}, u32[]{:S(2)}) copy-start(s32[2,64]{1,0:T(2,128)} %param.19) | copy-start | bytes 1540
  99.7 6.6 %copy-start.10 = (f32[2,64]{1,0:T(2,128)S(1)}, f32[2,64]{1,0:T(2,128)}, u32[]{:S(2)}) copy-start(f32[2,64]{1,0:T(2,128)} %param.18) | copy-start | bytes 1540
  99.7 7.2 %copy-start.11 = (f32[2,64]{1,0:T(2,128)S(1)}, f32[2,64]{1,0:T(2,128)}, u32[]{:S(2)}) copy-start(f32[2,64]{1,0:T(2,128)} %param.17) | copy-start | bytes 1540
  99.7 33.2 %copy-start.3 = (f32[64,768]{1,0:T(8,128)S(1)}, f32[64,768]{1,0:T(8,128)}, u32[]{:S(2)}) copy-start(f32[64,768]{1,0:T(8,128)} %param.15) | copy-start | bytes 589828
  106.1 86.2 %reduce-scatter.5.cloned.1.call-start = ((), (), s32[]{:S(2)}) async-start(), calls=%async_computation.4 | async-start | bytes 983040 | tf_op jit(solution)/shard_map/reduce_scatter | solution.py:71
  134.0 59.3 %copy-start.1 = (f32[64,768]{1,0:T(8,128)}, f32[64,768]{1,0:T(8,128)S(1)}, u32[]{:S(2)}) copy-start(f32[64,768]{1,0:T(8,128)S(1)} %multiply_add_fusion.2) | copy-start | bytes 589828
  134.0 58.3 %copy-start.2 = (f32[128,768]{1,0:T(8,128)S(1)}, f32[128,768]{1,0:T(8,128)}, u32[]{:S(2)}) copy-start(f32[128,768]{1,0:T(8,128)} %reduce-scatter.3.cloned.1.call-done) | copy-start | bytes 1179652
  134.0 58.3 %copy-start.4 = (f32[64,768]{1,0:T(8,128)S(1)}, f32[64,768]{1,0:T(8,128)}, u32[]{:S(2)}) copy-start(f32[64,768]{1,0:T(8,128)} %param.16) | copy-start | bytes 589828
Sparse Core Ops, SparseCore 0:
  15.3 75.5 all-gather.1
  106.3 26.5 reduce-scatter.2
  169.0 23.2 reduce-scatter.4
where the time goes:
time: 201 us
  waiting for transfers between devices  125 us (62%)
  blocking collectives  31.5 us (16%)
  between operations  14.1 us (7%)
  local copies, waits for them, and re-layouts  13.4 us (7%)
  other arithmetic  8.62 us (4%)
  matrix products  8.14 us (4%)
    all_gather x1, waiting for transfers between devices, shards(): gathered = lax.all_gather(packed, 'wide', axis=1, tiled=True)  75.4 us
    all_gather x1, blocking collectives, shards(): gathered_two = lax.all_gather(packed_two, 'wide', axis=1, tiled=True)  31.5 us
    reduce_scatter x1, waiting for transfers between devices, shards(): lax.psum_scatter(lax.dot_general(columns, prior_lt, (((0,), (0,)), ((), (...  25.9 us
    reduce_scatter x1, waiting for transfers between devices, shards(): lax.psum_scatter(lax.dot_general(columns, w_first, (((0,), (0,)), ((), ()...  23.3 us
    dot_general x1, matrix products, shards(): lax.dot_general(columns, prior_lt, (((0,), (0,)), ((), ())), precision=la...  6.42 us
    gather x1, local copies, waits for them, and re-layouts, shards(): chosen = jnp.take(gathered, slot, axis=1)  5.01 us
    unnamed x29, local copies, waits for them, and re-layouts  4.19 us
  transfers between devices with their start and end apart: 3, of which 3 were waited for; matrix products, arithmetic and copies ran while one was open for 0% of the time, Pallas kernels for 0%

commit v1 on v0

--- a/solution.py
+++ b/solution.py
@@ -4,6 +4,17 @@
 from jax.sharding import PartitionSpec as P
 
 P_SIZE = 256
+
+
+def gather_by_hops(x, axis, d):
+    devices = lax.axis_size(axis)
+    hops = [(i, (i + 1) % devices) for i in range(devices)]
+    parts = [x]
+    for far in range(1, devices):
+        parts = [lax.ppermute(parts[0], axis, hops), *parts]
+    whole = jnp.concatenate(parts, axis=d)
+    shift = (lax.axis_index(axis) + 1) * parts[-1].shape[d]
+    return jnp.roll(whole, shift, axis=d)
 
 
 def couple(block, diag, off, pairs):
@@ -65,7 +76,7 @@
     l_first = couple(w_first, inv_d[0], inv_e[0], panel_pairs[0])
     owner_two, rank_two, slot_two = slot_layout(second, tile_rows, capacity)
     packed_two = pack_local(l_first, second, owner_two, rank_two, here, tile_rows, capacity)
-    gathered_two = lax.all_gather(packed_two, "wide", axis=1, tiled=True)
+    gathered_two = gather_by_hops(packed_two, "wide", 1)
     crossed = jnp.take(gathered_two, slot_two, axis=1)
     columns = crossed
     correction = lax.psum_scatter(

time: 201 us -> 217 us (1.080)
  waiting for transfers between devices: 125 us -> 169 us
  blocking collectives: 31.5 us -> 0 us
    ppermute x0 -> x7, waiting for transfers between devices: none -> 47.8 us  [gather_by_hops(): parts = [lax.ppermute(parts[0], axis, hops), *parts]]
    all_gather x1 -> x0, blocking collectives: 31.5 us -> none  [shards(): gathered_two = lax.all_gather(packed_two, 'wide', axis=1, tiled=True)]
    reduce_scatter x1, waiting for transfers between devices: 23.3 us -> 19.4 us  [shards(): lax.psum_scatter(lax.dot_general(columns, w_first, (((0,), (0,)), ((), ()...]
  transfers between devices with their start and end apart: 3 -> 10, of which waited for: 3 -> 10; matrix products, arithmetic and copies ran while one was open for 0% -> 0% of each run, Pallas kernels for 0% -> 0%
where the time goes in v1:
time: 217 us
  waiting for transfers between devices  169 us (78%)
  between operations  14.3 us (7%)
  local copies, waits for them, and re-layouts  13.5 us (6%)
  other arithmetic  10.2 us (5%)
  matrix products  8.12 us (4%)
    all_gather x1, waiting for transfers between devices, shards(): gathered = lax.all_gather(packed, 'wide', axis=1, tiled=True)  75.4 us
    ppermute x7, waiting for transfers between devices, gather_by_hops(): parts = [lax.ppermute(parts[0], axis, hops), *parts]  47.8 us
    reduce_scatter x1, waiting for transfers between devices, shards(): lax.psum_scatter(lax.dot_general(columns, prior_lt, (((0,), (0,)), ((), (...  26.4 us
    reduce_scatter x1, waiting for transfers between devices, shards(): lax.psum_scatter(lax.dot_general(columns, w_first, (((0,), (0,)), ((), ()...  19.4 us
    dot_general x1, matrix products, shards(): lax.dot_general(columns, prior_lt, (((0,), (0,)), ((), ())), precision=la...  6.41 us
    gather x1, local copies, waits for them, and re-layouts, shards(): chosen = jnp.take(gathered, slot, axis=1)  5.01 us
  transfers between devices with their start and end apart: 10, of which 10 were waited for; matrix products, arithmetic and copies ran while one was open for 0% of the time, Pallas kernels for 0%

profile of v1, /device:TPU:0, one launch (start us, length us, event | category | flops | bytes accessed | tf_op | source)
XLA Modules:
  0.0 216.8 jit_solution(5872956812041997501)
XLA Ops:
  7.2 0.0 all-gather.2.cloned.1.call-start
  7.2 0.7 and_select_fusion
  7.9 0.7 broadcast_divide_fusion
  8.6 0.7 and_bitcast_fusion
  9.3 0.7 compare_reduce_fusion
  10.1 0.2 convert_reduce_fusion
  10.3 0.1 select_reduce_fusion
  10.5 0.1 fusion.2
  10.7 0.2 convert_reduce_fusion.1
  10.8 0.1 select_reduce_fusion.1
  11.0 2.4 %copy.17 = f32[1024,768]{0,1:T(8,128)S(1)} copy(f32[1024,768]{1,0:T(8,128)} %param.10) | data formatting | bytes 6291456 | tf_op args[0]
  13.4 1.6 gather_fusion
  15.0 2.0 select_bitcast_fusion.1
  17.0 0.0 reduce-scatter.3.cloned.1.call-start
  17.1 0.1 pad_maximum_fusion
  17.2 75.4 %all-gather.2.cloned.1.call-done = f32[1024,1024]{0,1:T(8,128)} async-done(((f32[1024,128]{0,1:T(8,128)}), f32[1024,1024]{0,1:T(8,128)}) %all-gather.2.cloned.1.call-update) | async-done | bytes 4194320 | tf_op jit(solution)/shard_map/all_gather | solution.py:58
  92.7 5.0 %gather_fusion.1 = f32[512,1024]{1,0:T(8,128)S(1)} fusion(f32[1024,1024]{0,1:T(8,128)} %all-gather.2.cloned.1.call-done, s32[1024]{0:T(1024)S(1)} %pad_clamp_fusion.2), kind=kCustom, calls=%fused_computation.1 | custom fusion | bytes 4196352 | tf_op jit(solution)/shard_map/jit(_take)/gather | solution.py:59
  97.7 0.2 select_bitcast_fusion
  97.9 0.8 fusion.18
  98.7 0.8 multiply_add_fusion
  99.6 0.1 copy.18
  99.7 1.7 copy-done
  101.5 6.4 %fusion.21 = f32[512,768]{1,0:T(8,128)} fusion(f32[1024,512]{0,1:T(8,128)S(1)} %bitcast.72, f32[1024,768]{1,0:T(8,128)S(1)} %copy-done), kind=kOutput, calls=%fused_computation.100 | convolution fusion | flops 4831838208 | bytes 6815744 | tf_op jit(solution)/shard_map/dot_general | solution.py:68
  107.9 0.0 reduce-scatter.5.cloned.1.call-start
  108.0 0.1 pad_maximum_fusion.2
  108.1 0.1 fusion.8
  108.2 26.4 %reduce-scatter.3.cloned.1.call-done = f32[128,768]{1,0:T(8,128)} async-done(((f32[512,768]{1,0:T(8,128)}), f32[128,768]{1,0:T(8,128)}) %reduce-scatter.3.cloned.1.call-update) | async-done | bytes 393232 | tf_op jit(solution)/shard_map/reduce_scatter | solution.py:67
  134.6 0.9 slice_subtract_fusion.1
  135.6 0.1 multiply_add_fusion.2
  135.7 0.2 copy.19
  135.9 0.6 gather_fusion.2
  136.5 0.1 select_bitcast_fusion.2
  136.6 1.5 collective-permute-start
  138.2 5.5 %collective-permute-done = f32[64,128]{0,1:T(8,128)S(1)} collective-permute-done((f32[64,128]{0,1:T(8,128)S(1)}, f32[64,128]{0,1:T(8,128)S(1)}, u32[]{:S(2)}, u32[]{:S(2)}) %collective-permute-start) | collective-permute-done | bytes 32800 | tf_op jit(solution)/shard_map/ppermute | solution.py:14
  143.7 7.0 %collective-permute-done.1 = f32[64,128]{0,1:T(8,128)S(1)} collective-permute-done((f32[64,128]{0,1:T(8,128)S(1)}, f32[64,128]{0,1:T(8,128)S(1)}, u32[]{:S(2)}, u32[]{:S(2)}) %collective-permute-start.1) | collective-permute-done | bytes 32800 | tf_op jit(solution)/shard_map/ppermute | solution.py:14
  150.6 7.0 %collective-permute-done.2 = f32[64,128]{0,1:T(8,128)S(1)} collective-permute-done((f32[64,128]{0,1:T(8,128)S(1)}, f32[64,128]{0,1:T(8,128)S(1)}, u32[]{:S(2)}, u32[]{:S(2)}) %collective-permute-start.2) | collective-permute-done | bytes 32800 | tf_op jit(solution)/shard_map/ppermute | solution.py:14
  157.6 7.0 %collective-permute-done.3 = f32[64,128]{0,1:T(8,128)S(1)} collective-permute-done((f32[64,128]{0,1:T(8,128)S(1)}, f32[64,128]{0,1:T(8,128)S(1)}, u32[]{:S(2)}, u32[]{:S(2)}) %collective-permute-start.3) | collective-permute-done | bytes 32800 | tf_op jit(solution)/shard_map/ppermute | solution.py:14
  164.6 7.6 %collective-permute-done.4 = f32[64,128]{0,1:T(8,128)S(1)} collective-permute-done((f32[64,128]{0,1:T(8,128)S(1)}, f32[64,128]{0,1:T(8,128)S(1)}, u32[]{:S(2)}, u32[]{:S(2)}) %collective-permute-start.4) | collective-permute-done | bytes 32800 | tf_op jit(solution)/shard_map/ppermute | solution.py:14
  172.1 6.9 %collective-permute-done.5 = f32[64,128]{0,1:T(8,128)S(1)} collective-permute-done((f32[64,128]{0,1:T(8,128)S(1)}, f32[64,128]{0,1:T(8,128)S(1)}, u32[]{:S(2)}, u32[]{:S(2)}) %collective-permute-start.5) | collective-permute-done | bytes 32800 | tf_op jit(solution)/shard_map/ppermute | solution.py:14
  179.1 6.9 %collective-permute-done.6 = f32[64,128]{0,1:T(8,128)S(1)} collective-permute-done((f32[64,128]{0,1:T(8,128)S(1)}, f32[64,128]{0,1:T(8,128)S(1)}, u32[]{:S(2)}, u32[]{:S(2)}) %collective-permute-start.6) | collective-permute-done | bytes 32800 | tf_op jit(solution)/shard_map/ppermute | solution.py:14
  186.1 0.1 constant_dynamic-update-slice_fusion.8
  186.4 0.1 constant_dynamic-update-slice_fusion
  186.5 0.7 gather_fusion.3
  187.3 1.7 fusion.5
  189.0 0.1 pad_maximum_fusion.1
  189.1 19.4 %reduce-scatter.5.cloned.1.call-done = f32[64,768]{1,0:T(8,128)} async-done(((f32[256,768]{1,0:T(8,128)}), f32[64,768]{1,0:T(8,128)}) %reduce-scatter.5.cloned.1.call-update) | async-done | bytes 196624 | tf_op jit(solution)/shard_map/reduce_scatter | solution.py:82
  208.5 1.0 fusion.4
  209.5 0.8 multiply_add_fusion.1
  (72 shorter events, 0.5 us)
Async XLA Ops:
  7.2 85.5 %all-gather.2.cloned.1.call-start = ((), (), s32[]{:S(2)}) async-start(), calls=%async_computation.2 | async-start | bytes 4718592 | tf_op jit(solution)/shard_map/all_gather | solution.py:58
  13.4 3.7 %copy-start.6 = (f32[1024]{0:T(1024)S(1)}, f32[1024]{0:T(1024)}, u32[]{:S(2)}) copy-start(f32[1024]{0:T(1024)} %param.12) | copy-start | bytes 12292
  13.4 3.7 %copy-start.7 = (s32[1024]{0:T(1024)S(1)}, s32[1024]{0:T(1024)}, u32[]{:S(2)}) copy-start(s32[1024]{0:T(1024)} %param.13) | copy-start | bytes 12292
  17.0 117.6 %reduce-scatter.3.cloned.1.call-start = ((), (), s32[]{:S(2)}) async-start(), calls=%async_computation.3 | async-start | bytes 1966080 | tf_op jit(solution)/shard_map/reduce_scatter | solution.py:67
  97.9 0.9 copy-start.5
  99.6 1.9 copy-start
  101.5 6.5 %copy-start.8 = (s32[2,64]{1,0:T(2,128)S(1)}, s32[2,64]{1,0:T(2,128)}, u32[]{:S(2)}) copy-start(s32[2,64]{1,0:T(2,128)} %param.19) | copy-start | bytes 1540
  101.5 6.5 %copy-start.9 = (f32[2,64]{1,0:T(2,128)S(1)}, f32[2,64]{1,0:T(2,128)}, u32[]{:S(2)}) copy-start(f32[2,64]{1,0:T(2,128)} %param.18) | copy-start | bytes 1540
  101.5 6.7 %copy-start.10 = (f32[2,64]{1,0:T(2,128)S(1)}, f32[2,64]{1,0:T(2,128)}, u32[]{:S(2)}) copy-start(f32[2,64]{1,0:T(2,128)} %param.17) | copy-start | bytes 1540
  101.5 33.1 %copy-start.3 = (f32[64,768]{1,0:T(8,128)S(1)}, f32[64,768]{1,0:T(8,128)}, u32[]{:S(2)}) copy-start(f32[64,768]{1,0:T(8,128)} %param.15) | copy-start | bytes 589828
  107.9 100.6 %reduce-scatter.5.cloned.1.call-start = ((), (), s32[]{:S(2)}) async-start(), calls=%async_computation.4 | async-start | bytes 983040 | tf_op jit(solution)/shard_map/reduce_scatter | solution.py:82
  135.7 50.8 %copy-start.1 = (f32[64,768]{1,0:T(8,128)}, f32[64,768]{1,0:T(8,128)S(1)}, u32[]{:S(2)}) copy-start(f32[64,768]{1,0:T(8,128)S(1)} %multiply_add_fusion.2) | copy-start | bytes 589828
  136.6 7.0 %collective-permute-start = (f32[64,128]{0,1:T(8,128)S(1)}, f32[64,128]{0,1:T(8,128)S(1)}, u32[]{:S(2)}, u32[]{:S(2)}) collective-permute-start(f32[64,128]{0,1:T(8,128)S(1)} %select_bitcast_fusion.2), channel_id=1, source_target_pairs={{0,4},{4,8},{8,12},{12,16},{16,20},{20,24},{24,28},{28,0},{1,5},{5... | collective-permute-start | bytes 98312 | tf_op jit(solution)/shard_map/ppermute | solution.py:14
  143.7 7.0 %collective-permute-start.1 = (f32[64,128]{0,1:T(8,128)S(1)}, f32[64,128]{0,1:T(8,128)S(1)}, u32[]{:S(2)}, u32[]{:S(2)}) collective-permute-start(f32[64,128]{0,1:T(8,128)S(1)} %collective-permute-done), channel_id=1, source_target_pairs={{0,4},{4,8},{8,12},{12,16},{16,20},{20,24},{24,28},{28,0},{1,5},{5... | collective-permute-start | bytes 98312 | tf_op jit(solution)/shard_map/ppermute | solution.py:14
  150.6 7.0 %collective-permute-start.2 = (f32[64,128]{0,1:T(8,128)S(1)}, f32[64,128]{0,1:T(8,128)S(1)}, u32[]{:S(2)}, u32[]{:S(2)}) collective-permute-start(f32[64,128]{0,1:T(8,128)S(1)} %collective-permute-done.1), channel_id=1, source_target_pairs={{0,4},{4,8},{8,12},{12,16},{16,20},{20,24},{24,28},{28,0},{1,5},{5... | collective-permute-start | bytes 98312 | tf_op jit(solution)/shard_map/ppermute | solution.py:14
  157.6 7.0 %collective-permute-start.3 = (f32[64,128]{0,1:T(8,128)S(1)}, f32[64,128]{0,1:T(8,128)S(1)}, u32[]{:S(2)}, u32[]{:S(2)}) collective-permute-start(f32[64,128]{0,1:T(8,128)S(1)} %collective-permute-done.2), channel_id=1, source_target_pairs={{0,4},{4,8},{8,12},{12,16},{16,20},{20,24},{24,28},{28,0},{1,5},{5... | collective-permute-start | bytes 98312 | tf_op jit(solution)/shard_map/ppermute | solution.py:14
  164.5 7.6 %collective-permute-start.4 = (f32[64,128]{0,1:T(8,128)S(1)}, f32[64,128]{0,1:T(8,128)S(1)}, u32[]{:S(2)}, u32[]{:S(2)}) collective-permute-start(f32[64,128]{0,1:T(8,128)S(1)} %collective-permute-done.3), channel_id=1, source_target_pairs={{0,4},{4,8},{8,12},{12,16},{16,20},{20,24},{24,28},{28,0},{1,5},{5... | collective-permute-start | bytes 98312 | tf_op jit(solution)/shard_map/ppermute | solution.py:14
  172.1 7.0 %collective-permute-start.5 = (f32[64,128]{0,1:T(8,128)S(1)}, f32[64,128]{0,1:T(8,128)S(1)}, u32[]{:S(2)}, u32[]{:S(2)}) collective-permute-start(f32[64,128]{0,1:T(8,128)S(1)} %collective-permute-done.4), channel_id=1, source_target_pairs={{0,4},{4,8},{8,12},{12,16},{16,20},{20,24},{24,28},{28,0},{1,5},{5... | collective-permute-start | bytes 98312 | tf_op jit(solution)/shard_map/ppermute | solution.py:14
  179.1 7.0 %collective-permute-start.6 = (f32[64,128]{0,1:T(8,128)S(1)}, f32[64,128]{0,1:T(8,128)S(1)}, u32[]{:S(2)}, u32[]{:S(2)}) collective-permute-start(f32[64,128]{0,1:T(8,128)S(1)} %collective-permute-done.5), channel_id=1, source_target_pairs={{0,4},{4,8},{8,12},{12,16},{16,20},{20,24},{24,28},{28,0},{1,5},{5... | collective-permute-start | bytes 98312 | tf_op jit(solution)/shard_map/ppermute | solution.py:14
  186.3 22.2 %copy-start.2 = (f32[128,768]{1,0:T(8,128)S(1)}, f32[128,768]{1,0:T(8,128)}, u32[]{:S(2)}) copy-start(f32[128,768]{1,0:T(8,128)} %reduce-scatter.3.cloned.1.call-done) | copy-start | bytes 1179652
  186.3 22.2 %copy-start.4 = (f32[64,768]{1,0:T(8,128)S(1)}, f32[64,768]{1,0:T(8,128)}, u32[]{:S(2)}) copy-start(f32[64,768]{1,0:T(8,128)} %param.16) | copy-start | bytes 589828
Sparse Core Ops, SparseCore 0:
  17.1 75.5 all-gather.1
  108.0 26.5 reduce-scatter.2
  189.1 19.3 reduce-scatter.4
